TPU v7x, 256 devices: a whole 4x4x8 slice. The times are simulated.
256 devices in a mesh: group: 16 (over y_lo, x, core), fsdp: 16 (over y_hi, z).
Axes of the slice: x: 4, y: 4 (y_hi: 2, y_lo: 2; y = y_hi * 2 + y_lo), z: 8, core: 2. Of those that a mesh axis runs over, the one named last changes fastest.
Arguments:
- activations: bfloat16 [16, 6144, 8192], P('group', 'fsdp'), may hold values from -6 to 6
- key_cotangent: bfloat16 [16, 6144, 512], P('group', 'fsdp'), may hold values from -0.079589844 to 0.079589844
- master: float32 [16, 8192, 512], P('group', 'fsdp'), may hold values from -6 to 6
- first_codes: bfloat16 [16, 8192, 512], P('group', 'fsdp'), may hold values from -1 to 1
- first_scales: float32 [16, 8192, 4], P('group', 'fsdp'), may hold values from 0.03 to 0.3
- second_codes: bfloat16 [16, 8192, 512], P('group', 'fsdp'), may hold values from 0.049804688 to 1
- second_scales: float32 [16, 8192, 4], P('group', 'fsdp'), may hold values from 0.2 to 3
- partner: int32 [16], replicated, may hold values from 0 to 15, as said below
Outputs:
- master_out: float32 [16, 8192, 512], P('group', 'fsdp')
- first_codes_out: bfloat16 [16, 8192, 512], P('group', 'fsdp')
- first_scales_out: float32 [16, 8192, 4], P('group', 'fsdp')
- second_codes_out: bfloat16 [16, 8192, 512], P('group', 'fsdp')
- second_scales_out: float32 [16, 8192, 4], P('group', 'fsdp')
Inputs may be any that keep to these rules, and one draw needn't show every extreme that they name: partner is a matching: partner[partner[g]] == g and partner[g] != g for every group g.
All inputs are finite; a program needn't handle non-finite values. Where the computation divides by a largest or mean magnitude, that divisor is 1e-20 or more.
Results may differ from a plain program's by a relative error of at most 0.0085.
Values may be sent and summed in bfloat16 or wider, within the bound.
A program may use at most 128 MiB of HBM per device.

v0:
```python
import math

import jax
import jax.numpy as jnp
from jax import lax
from jax.sharding import PartitionSpec as P

beta_one = 0.9
beta_two = 0.95
learn_rate = 0.01
decay_rate = 0.1
adam_epsilon = 1e-08
block_epsilon = 1e-06


def side_by_side(arrays, axis, split_dim, concat_dim, along):
    widths = [math.prod(a.shape[along:]) for a in arrays]
    both = jnp.concatenate(
        [a.reshape(*a.shape[:along], w) for a, w in zip(arrays, widths)], axis=along
    )
    result = lax.all_to_all(both, axis, split_axis=split_dim, concat_axis=concat_dim, tiled=True)
    parts = jnp.split(result, [sum(widths[:k]) for k in range(1, len(widths))], axis=along)
    return tuple(
        (b.reshape(*result.shape[:along], *a.shape[along:]) for a, b in zip(arrays, parts))
    )


def side_by_side_2(arrays, axis, split_dim, concat_dim, along):
    widths = [a.shape[along] for a in arrays]
    both = jnp.concatenate(arrays, axis=along)
    result = lax.all_to_all(both, axis, split_axis=split_dim, concat_axis=concat_dim, tiled=True)
    return tuple(jnp.split(result, [sum(widths[:k]) for k in range(1, len(widths))], axis=along))


def row_quantize(values):
    scales = jnp.max(jnp.abs(values), axis=-1) + block_epsilon
    codes = (values / scales[..., None]).astype(jnp.bfloat16)
    return (codes, scales)


def row_dequantize(codes, scales):
    return codes.astype(jnp.float32) * scales[..., None]


def pair_mean(matching, values):
    other = jnp.einsum("hk,krc->hrc", matching, values, precision=lax.Precision.HIGHEST)
    return (values + other) / 2.0


def send_back(master_rows, first_codes, first_scales, second_codes, second_scales):
    state = side_by_side((master_rows, first_scales, second_scales), "group", 0, 0, 2)
    codes = side_by_side_2((first_codes, second_codes), "group", 0, 0, 1)
    return (state, codes)


def per_device(
    activations,
    key_cotangent,
    master,
    first_codes,
    first_scales,
    second_codes,
    second_scales,
    partner,
):
    inputs = activations[0]
    cotangent = key_cotangent[0]
    own_rows = master.shape[1]
    width = master.shape[2]
    groups = lax.axis_size("group")
    contract = (((0,), (0,)), ((), ()))
    columns = lax.all_to_all(inputs, "fsdp", split_axis=1, concat_axis=0, tiled=True)
    grad = lax.dot_general(
        columns,
        lax.all_gather(cotangent, "fsdp", axis=0, tiled=True),
        contract,
        preferred_element_type=jnp.float32,
    )
    block_rows = own_rows * width // 128
    piece_rows = block_rows // groups
    first_old = row_dequantize(
        first_codes[0].reshape(block_rows, 128), first_scales[0].reshape(block_rows)
    )
    second_old = row_dequantize(
        second_codes[0].reshape(block_rows, 128), second_scales[0].reshape(block_rows)
    )
    gradient_rows = grad.reshape(block_rows, 128)
    master_rows = master[0].reshape(block_rows, 128)
    first = beta_one * first_old + (1.0 - beta_one) * gradient_rows
    second = beta_two * second_old + (1.0 - beta_two) * gradient_rows * gradient_rows
    updated = master_rows - learn_rate * (
        first / (jnp.sqrt(second) + adam_epsilon) + decay_rate * master_rows
    )
    first_mid_codes, first_mid_scales = row_quantize(first)
    second_mid_codes, second_mid_scales = row_quantize(second)
    updated = updated.reshape(groups, piece_rows, 128)
    first_mid_codes = first_mid_codes.reshape(groups, piece_rows, 128)
    second_mid_codes = second_mid_codes.reshape(groups, piece_rows, 128)
    first_mid_scales = first_mid_scales.reshape(groups, piece_rows)
    second_mid_scales = second_mid_scales.reshape(groups, piece_rows)
    first_plain = row_dequantize(first_mid_codes, first_mid_scales)
    second_plain = row_dequantize(second_mid_codes, second_mid_scales)
    spread_master, spread_first, spread_second = side_by_side_2(
        (updated, first_plain, second_plain), "group", 0, 0, 1
    )
    matching = (partner[:, None] == jnp.arange(groups, dtype=jnp.int32)[None, :]).astype(
        jnp.float32
    )
    master_mean = pair_mean(matching, spread_master)
    first_avg = pair_mean(matching, spread_first)
    second_avg = pair_mean(matching, spread_second)
    first_new_codes, first_new_scales = row_quantize(first_avg)
    second_new_codes, second_new_scales = row_quantize(second_avg)
    state, codes = send_back(
        master_mean, first_new_codes, first_new_scales, second_new_codes, second_new_scales
    )
    master_back, first_scales_back, second_scales_back = state
    first_codes_back, second_codes_back = codes
    master_out = master_back.reshape(1, own_rows, width)
    first_codes_out = first_codes_back.reshape(1, own_rows, width)
    second_codes_out = second_codes_back.reshape(1, own_rows, width)
    first_scales_out = first_scales_back.reshape(1, own_rows, width // 128)
    second_scales_out = second_scales_back.reshape(1, own_rows, width // 128)
    return (master_out, first_codes_out, first_scales_out, second_codes_out, second_scales_out)


def solution(mesh):
    return jax.shard_map(
        per_device,
        mesh=mesh,
        in_specs=(
            P("group", "fsdp", None),
            P("group", "fsdp", None),
            P("group", "fsdp", None),
            P("group", "fsdp", None),
            P("group", "fsdp", None),
            P("group", "fsdp", None),
            P("group", "fsdp", None),
            P(),
        ),
        out_specs=(
            P("group", "fsdp", None),
            P("group", "fsdp", None),
            P("group", "fsdp", None),
            P("group", "fsdp", None),
            P("group", "fsdp", None),
        ),
        check_vma=False,
    )
```

profile of v0, /device:TPU:1, one launch (start us, length us, event | category | flops | bytes accessed | tf_op | source)
XLA Modules:
  0.0 355.6 jit_solution(17866508978038156408)
XLA Ops:
  7.2 8.6 %copy.70 = bf16[1,384,8192]{1,2,0:T(8,128)(2,1)} copy(bf16[1,384,8192]{2,1,0:T(8,128)(2,1)} %param.8) | data formatting | bytes 12582912 | tf_op args[0]
  15.8 0.0 copy-start.3
  15.8 0.0 copy-start.4
  15.8 0.0 copy-start.1
  15.8 11.9 %all-to-all-start = ((bf16[384,16,512]{0,2,1:T(8,128)(2,1)}), bf16[384,16,512]{0,2,1:T(8,128)(2,1)}, u32[]{:S(2)}, u32[]{:S(2)}) async-start(bf16[384,16,512]{0,2,1:T(8,128)(2,1)} %bitcast.24), calls=%async_computation | async-start | bytes 12582912 | tf_op jit(solution)/shard_map/all_to_all | solution.py:72
  27.7 0.0 copy-start.2
  27.7 0.0 all-gather.3.cloned.1.call-start
  27.8 0.7 all-gather.3.cloned.1.call-update
  28.5 0.0 copy-done.3
  28.5 0.1 copy.69
  28.6 0.2 mul.154
  28.8 0.2 mul.137
  29.0 0.0 copy-done.4
  29.0 0.1 copy.72
  29.1 0.2 mul.161
  29.3 0.2 mul.143
  29.5 0.0 copy-done.1
  29.5 1.3 reshape.153
  30.7 0.3 reshape.151
  31.0 0.0 copy-done.2
  31.0 1.3 reshape.154
  32.3 0.3 reshape.152
  32.6 1.3 reshape_squeeze.2
  33.9 157.2 %all-to-all-done = bf16[384,16,512]{0,2,1:T(8,128)(2,1)} async-done(((bf16[384,16,512]{0,2,1:T(8,128)(2,1)}), bf16[384,16,512]{0,2,1:T(8,128)(2,1)}, u32[]{:S(2)}, u32[]{:S(2)}) %all-to-all-start) | async-done | bytes 6291488 | tf_op jit(solution)/shard_map/all_to_all | solution.py:72
  191.0 8.6 %copy.71 = bf16[16,384,512]{2,1,0:T(8,128)(2,1)} copy(bf16[16,384,512]{1,2,0:T(8,128)(2,1)} %bitcast.1) | data formatting | bytes 12582912 | tf_op jit(solution)/shard_map/all_to_all | solution.py:72
  199.7 35.6 %all-gather.3.cloned.1.call-done = bf16[1,6144,512]{2,1,0:T(8,128)(2,1)} async-done(((bf16[1,384,512]{2,1,0:T(8,128)(2,1)}), bf16[1,6144,512]{2,1,0:T(8,128)(2,1)}) %all-gather.3.cloned.1.call-update) | async-done | bytes 6291472 | tf_op jit(solution)/shard_map/all_gather | solution.py:75
  235.2 9.0 %fusion = f32[512,512]{1,0:T(8,128)} fusion(bf16[6144,512]{1,0:T(8,128)(2,1)} %bitcast.25, bf16[1,6144,512]{2,1,0:T(8,128)(2,1)} %all-gather.3.cloned.1.call-done), kind=kOutput, calls=%fused_computation | convolution fusion | flops 3221225472 | bytes 13631488 | tf_op jit(solution)/shard_map/dot_general | solution.py:73
  244.2 2.3 reshape.147
  246.6 2.3 reshape.146
  248.8 0.0 copy-start
  248.8 2.7 abs_reduce_fusion.2
  251.6 0.0 copy-done
  251.6 1.5 multiply_subtract_fusion
  253.1 0.3 pad_maximum_fusion
  253.4 42.7 %all_to_all.34 = f32[16,384,128]{2,1,0:T(8,128)S(1)} all-to-all(f32[16,384,128]{2,1,0:T(8,128)S(1)} %pad_maximum_fusion), channel_id=1, replica_groups=mesh['group'=16,'fsdp'=16] {'group'}, dimensions={0} | all-to-all | bytes 6291456 | tf_op jit(solution)/shard_map/all_to_all | solution.py:31
  296.1 0.0 copy-start.5
  296.1 0.3 fusion.21
  296.4 0.4 copy-done.5
  296.7 2.0 abs_reduce_fusion.1
  298.8 2.0 abs_reduce_fusion
  300.8 0.3 divide_convert_fusion.1
  301.2 0.3 divide_convert_fusion
  301.5 0.1 pad_maximum_fusion.2
  301.6 1.3 copy.84
  302.9 5.5 %all-to-all-start.3 = ((bf16[16,256,128]{2,1,0:T(8,128)(2,1)}), bf16[16,256,128]{2,1,0:T(8,128)(2,1)}, u32[]{:S(2)}, u32[]{:S(2)}) async-start(bf16[16,256,128]{2,1,0:T(8,128)(2,1)} %copy.84), calls=%async_computation.3 | async-start | bytes 2097152 | tf_op jit(solution)/shard_map/all_to_all | solution.py:31
  308.4 0.8 copy.80
  309.2 1.8 copy.81
  311.0 1.8 fusion.2
  312.8 1.6 pad_maximum_fusion.1
  314.4 1.7 copy.82
  316.1 8.2 %all-to-all-done.3 = bf16[16,256,128]{2,1,0:T(8,128)(2,1)} async-done(((bf16[16,256,128]{2,1,0:T(8,128)(2,1)}), bf16[16,256,128]{2,1,0:T(8,128)(2,1)}, u32[]{:S(2)}, u32[]{:S(2)}) %all-to-all-start.3) | async-done | bytes 1048608 | tf_op jit(solution)/shard_map/all_to_all | solution.py:31
  324.4 4.3 %all-to-all-start.2 = ((f32[16,128,130]{1,2,0:T(8,128)}), f32[16,128,130]{1,2,0:T(8,128)S(1)}, u32[]{:S(2)}, u32[]{:S(2)}) async-start(f32[16,128,130]{1,2,0:T(8,128)} %copy.82), calls=%async_computation.2 | async-start | bytes 2228224 | tf_op jit(solution)/shard_map/all_to_all | solution.py:21
  328.6 1.3 fusion.22
  329.9 1.1 reshape.149
  331.0 1.1 reshape.150
  332.1 13.1 %all-to-all-done.2 = f32[16,128,130]{1,2,0:T(8,128)S(1)} async-done(((f32[16,128,130]{1,2,0:T(8,128)}), f32[16,128,130]{1,2,0:T(8,128)S(1)}, u32[]{:S(2)}, u32[]{:S(2)}) %all-to-all-start.2) | async-done | bytes 1064992 | tf_op jit(solution)/shard_map/all_to_all | solution.py:21
  345.2 0.1 split.35
  345.3 0.3 copy.83
  345.6 1.1 reshape.148
  346.8 0.3 reshape_reshape.6
  347.1 0.7 copy.85
  347.8 0.3 reshape_reshape.7
  348.0 0.7 copy.86
  (4 shorter events, 0.1 us)
Async XLA Ops:
  15.8 12.7 %copy-start.3 = (f32[1,512,4]{1,2,0:T(4,128)S(1)}, f32[1,512,4]{1,2,0:T(4,128)}, u32[]{:S(2)}) copy-start(f32[1,512,4]{1,2,0:T(4,128)} %param.12) | copy-start | bytes 24580
  15.8 13.2 %copy-start.4 = (f32[1,512,4]{1,2,0:T(4,128)S(1)}, f32[1,512,4]{1,2,0:T(4,128)}, u32[]{:S(2)}) copy-start(f32[1,512,4]{1,2,0:T(4,128)} %param.14) | copy-start | bytes 24580
  15.8 13.7 %copy-start.1 = (bf16[1,512,512]{2,1,0:T(8,128)(2,1)S(1)}, bf16[1,512,512]{2,1,0:T(8,128)(2,1)}, u32[]{:S(2)}) copy-start(bf16[1,512,512]{2,1,0:T(8,128)(2,1)} %param.11) | copy-start | bytes 1572868
  15.8 175.3 %all-to-all-start = ((bf16[384,16,512]{0,2,1:T(8,128)(2,1)}), bf16[384,16,512]{0,2,1:T(8,128)(2,1)}, u32[]{:S(2)}, u32[]{:S(2)}) async-start(bf16[384,16,512]{0,2,1:T(8,128)(2,1)} %bitcast.24), calls=%async_computation | async-start | bytes 12582912 | tf_op jit(solution)/shard_map/all_to_all | solution.py:72
  27.7 3.3 copy-start.2
  27.7 207.5 %all-gather.3.cloned.1.call-start = ((), (), s32[]{:S(2)}) async-start(), calls=%async_computation.4 | async-start | bytes 6684672 | tf_op jit(solution)/shard_map/all_gather | solution.py:75
  248.8 2.8 copy-start
  296.1 0.7 copy-start.5
  302.9 21.5 %all-to-all-start.3 = ((bf16[16,256,128]{2,1,0:T(8,128)(2,1)}), bf16[16,256,128]{2,1,0:T(8,128)(2,1)}, u32[]{:S(2)}, u32[]{:S(2)}) async-start(bf16[16,256,128]{2,1,0:T(8,128)(2,1)} %copy.84), calls=%async_computation.3 | async-start | bytes 2097152 | tf_op jit(solution)/shard_map/all_to_all | solution.py:31
  324.4 20.8 %all-to-all-start.2 = ((f32[16,128,130]{1,2,0:T(8,128)}), f32[16,128,130]{1,2,0:T(8,128)S(1)}, u32[]{:S(2)}, u32[]{:S(2)}) async-start(f32[16,128,130]{1,2,0:T(8,128)} %copy.82), calls=%async_computation.2 | async-start | bytes 2228224 | tf_op jit(solution)/shard_map/all_to_all | solution.py:21
Sparse Core Ops, SparseCore 0:
  31.1 204.0 all-gather.2
where the time goes:
time: 357 us; the launch traced here: 356 us
  waiting for transfers between devices  215 us (60%)
  blocking collectives  42.7 us (12%)
  local copies, waits for them, and re-layouts  40.4 us (11%)
  starting transfers between devices  21.7 us (6%)
  matrix products  14.9 us (4%)
  between operations  14.3 us (4%)
  other arithmetic  6.93 us (2%)
    all_to_all x1, waiting for transfers between devices, per_device(): lax.all_to_all(inputs, 'fsdp', split_axis=1, concat_axis=0, tiled=True)  157 us
    all_to_all x1, blocking collectives, side_by_side_2(): lax.all_to_all(both, axis, split_axis=split_dim, concat_axis=concat_dim,...  42.7 us
    all_gather x1, waiting for transfers between devices, per_device(): lax.all_gather(cotangent, 'fsdp', axis=0, tiled=True)  35.6 us
    all_to_all x1, waiting for transfers between devices, side_by_side(): lax.all_to_all(both, axis, split_axis=split_dim, concat_axis=concat_dim,...  13.1 us
    all_to_all x1, starting transfers between devices, per_device(): lax.all_to_all(inputs, 'fsdp', split_axis=1, concat_axis=0, tiled=True)  11.9 us
    unnamed x17, local copies, waits for them, and re-layouts  10.7 us
    dot_general x1, matrix products, per_device(): lax.dot_general(columns, lax.all_gather(cotangent, 'fsdp', axis=0, tiled=...  9.01 us
    all_to_all x1, local copies, waits for them, and re-layouts, per_device(): lax.all_to_all(inputs, 'fsdp', split_axis=1, concat_axis=0, tiled=True)  8.61 us
  transfers between devices with their start and end apart: 4, of which 4 were waited for; matrix products, arithmetic and copies ran while one was open for 7% of the time, Pallas kernels for 0%

commit v1 on v0

v1 whole, which is shorter than its diff:
```python
import jax
import jax.numpy as jnp
from jax import lax
from jax.experimental import pallas as pl
from jax.experimental.pallas import tpu as pltpu
from jax.sharding import PartitionSpec as P

beta_one = 0.9
beta_two = 0.95
learn_rate = 0.01
decay_rate = 0.1
adam_epsilon = 1e-08
block_epsilon = 1e-06

NG = 16
NZ = 8
T = 384
W = 512
Q = 4
R = W // Q
NP = 7 * Q
PARTS = 2
PR = W // PARTS
MR = PR // NG
SR = W // NG
BLK = 128
NB = W // BLK
MESH = pl.DeviceIdType.MESH
F32 = jnp.float32
BF16 = jnp.bfloat16


def kernel(
    partner_ref, x_hbm, c_hbm, m_hbm, c1_hbm, c2_hbm, s1_hbm, s2_hbm,
    mo_hbm, c1o_hbm, so1_hbm, c2o_hbm, so2_hbm,
    xv, cv, mv, sbuf, rbuf, ysb, yrb,
    st, st_r, st_b, st_p, sc, sc_all, srow,
    f1, f2, mm, grad, gs, gr0, gr1, gb, gp, mid1, mid2, upd,
    mo, c1o, c2o, so,
    x_sem, in_sem, out_sem, zs_sem, zr_sem, ys_sem, yr_sem,
    ss_sem, sr_sem, cs_sem, cr_sem, ps_sem, pr_sem, gs_sem, gr_sem, hs_sem, hr_sem,
):
    g = lax.axis_index("group")
    f_me = lax.axis_index("fsdp")
    z = f_me % NZ
    yh = f_me // NZ
    y_other = 1 - yh
    up = (g, yh * NZ + (z + 1) % NZ)
    down = (g, yh * NZ + (z + NZ - 1) % NZ)
    across = (g, y_other * NZ + z)

    def member(r):
        return (g + r) % NG

    def x_copy(f):
        cols = pl.ds(pl.multiple_of(f * W, W), W)
        return pltpu.make_async_copy(x_hbm.at[:, cols], xv.at[f], x_sem.at[f])

    def chunk(y, t):
        return y * NZ + t

    far = (z + 4) % NZ
    first_chunks = [
        chunk(y_other, far), chunk(yh, far),
        chunk(yh, (z + 3) % NZ), chunk(y_other, (z + 5) % NZ),
    ]
    c_in = pltpu.make_async_copy(c_hbm, cv, in_sem.at[0])
    c_in.start()
    for f in first_chunks:
        x_copy(f).start()
    state_in = [
        pltpu.make_async_copy(m_hbm, mv, in_sem.at[1]),
        pltpu.make_async_copy(c1_hbm, st.at[:, 1], in_sem.at[2]),
        pltpu.make_async_copy(c2_hbm, st.at[:, 2], in_sem.at[3]),
        pltpu.make_async_copy(s1_hbm, sc.at[pl.ds(0, NB)], in_sem.at[4]),
        pltpu.make_async_copy(s2_hbm, sc.at[pl.ds(NB, NB)], in_sem.at[5]),
    ]
    rest = [chunk(yh, (z + 5) % NZ), chunk(y_other, (z + 3) % NZ)]
    for d in (2, 6, 1, 7, 0):
        rest += [chunk(y_other, (z + d) % NZ), chunk(yh, (z + d) % NZ)]
    for f in rest[:2]:
        x_copy(f).start()
    for c in state_in:
        c.start()
    for f in rest[2:]:
        x_copy(f).start()

    barrier = pltpu.get_barrier_semaphore()
    for d in (up, down, across):
        pl.semaphore_signal(barrier, inc=1, device_id=d, device_id_type=MESH)

    def greet(r, _):
        pl.semaphore_signal(barrier, inc=1, device_id=(member(r), f_me), device_id_type=MESH)
        return 0

    lax.fori_loop(1, NG, greet, 0)

    def partial_grad(f, q):
        cols = pl.ds(pl.multiple_of(q * R, R), R)
        return lax.dot_general(
            xv[f, :, cols], cv[...], (((0,), (0,)), ((), ())), preferred_element_type=F32
        )

    def ring_copy(way, n):
        return pltpu.make_async_remote_copy(
            src_ref=sbuf.at[way, n], dst_ref=rbuf.at[way, n],
            send_sem=zs_sem.at[way, n], recv_sem=zr_sem.at[way, n],
            device_id=(up, down)[way], device_id_type=MESH,
        )

    def ring_piece(way, n, fresh):
        m = n + Q
        step, p = m // (2 * Q), m % (2 * Q)
        q, half = p % Q, p // Q
        d = 4 - step
        last = step // 3
        if way == 0:
            kind = half + (1 - 2 * half) * (1 - last)
            t = (z + d) % NZ
            prev = n - 2 * Q + last * (Q - 2 * Q * half)
        else:
            kind = half
            t = (z + NZ - d) % NZ
            prev = n - 2 * Q
        y = yh * kind + y_other * (1 - kind)
        f = chunk(y, t)
        total = partial_grad(f, q)
        if not fresh:
            ring_copy(way, prev).wait_recv()
            total = total + rbuf[way, prev].astype(F32)
        sbuf[way, n] = total.astype(BF16)
        ring_copy(way, n).start()

    def fresh_step(n, _):
        ring_piece(0, n, True)
        ring_piece(1, n, True)
        return 0

    def ring_step(n, _):
        ring_piece(0, n, False)
        ring_piece(1, n, False)
        return 0

    c_in.wait()
    x_copy(first_chunks[0]).wait()
    x_copy(first_chunks[1]).wait()
    pl.semaphore_wait(barrier, NG + 2)
    lax.fori_loop(0, Q, fresh_step, 0)
    x_copy(first_chunks[2]).wait()
    x_copy(first_chunks[3]).wait()
    lax.fori_loop(Q, 2 * Q, fresh_step, 0)

    for c in state_in:
        c.wait()
    for f in rest:
        x_copy(f).wait()

    def to_bf16(j, _):
        st[j, 0] = mv[j].astype(BF16)
        return 0

    lax.fori_loop(0, NG, to_bf16, 0)

    def spread_copy(r, src, dst, s_sem, r_sem):
        return pltpu.make_async_remote_copy(
            src_ref=src, dst_ref=dst, send_sem=s_sem, recv_sem=r_sem,
            device_id=(member(r), f_me), device_id_type=MESH,
        )

    def state_out(r):
        return spread_copy(r, st.at[member(r)], st_r.at[g], ss_sem.at[r], sr_sem.at[r])

    def scale_out(r):
        return spread_copy(r, sc, sc_all.at[g], cs_sem.at[r], cr_sem.at[r])

    def state_back(r):
        return spread_copy(r, st_b.at[member(r)], st_p.at[g], ps_sem.at[r], pr_sem.at[r])

    def each_member(fn):
        def body(r, _):
            fn(r)
            return 0

        lax.fori_loop(1, NG, body, 0)

    def start_state(r):
        state_out(r).start()
        scale_out(r).start()

    each_member(start_state)
    st_r[g] = st[g]
    sc_all[g] = sc[...]

    lax.fori_loop(2 * Q, 4 * Q, ring_step, 0)

    def state_arrived(r):
        state_out(r).wait_recv()
        scale_out(r).wait_recv()

    each_member(state_arrived)

    def select_state(h, _):
        st_b[h] = st_r[partner_ref[h]]
        return 0

    lax.fori_loop(0, NG, select_state, 0)
    each_member(lambda r: state_back(r).start())
    st_p[g] = st_b[g]

    lax.fori_loop(4 * Q, 5 * Q, ring_step, 0)

    each_member(lambda r: state_back(r).wait_recv())
    srow[0] = jnp.transpose(sc[...])
    srow[1] = jnp.transpose(sc_all[partner_ref[g]])

    def prepare(j, _):
        rows = pl.ds(pl.multiple_of(j * SR, SR), SR)
        own_s, other_s = srow[0, rows, :], srow[1, rows, :]
        for b in range(NB):
            lanes = slice(b * BLK, (b + 1) * BLK)
            for who, buf, s in ((0, st, own_s), (1, st_p, other_s)):
                f1[who, rows, lanes] = beta_one * (buf[j, 1, :, lanes].astype(F32) * s[:, b : b + 1])
                f2[who, rows, lanes] = beta_two * (
                    buf[j, 2, :, lanes].astype(F32) * s[:, NB + b : NB + b + 1]
                )
        mm[rows, :] = (0.5 * (1.0 - learn_rate * decay_rate)) * (mv[j] + st_p[j, 0].astype(F32))
        return 0

    lax.fori_loop(0, NG, prepare, 0)

    lax.fori_loop(5 * Q, NP, ring_step, 0)

    def across_copy(q):
        return pltpu.make_async_remote_copy(
            src_ref=ysb.at[q], dst_ref=yrb.at[q], send_sem=ys_sem.at[q], recv_sem=yr_sem.at[q],
            device_id=across, device_id_type=MESH,
        )

    def plane_sum(y, n, q):
        total = partial_grad(chunk(y, z), q)
        ring_copy(0, n).wait_recv()
        ring_copy(1, n).wait_recv()
        return total + rbuf[0, n].astype(F32) + rbuf[1, n].astype(F32)

    def other_plane(q, _):
        ysb[q] = plane_sum(y_other, 5 * Q + q, q).astype(BF16)
        across_copy(q).start()
        return 0

    lax.fori_loop(0, Q, other_plane, 0)

    gr = (gr0, gr1)

    def grad_out(k, r):
        return spread_copy(r, gs.at[k, member(r)], gr[k].at[g], gs_sem.at[k, r], gr_sem.at[k, r])

    def grad_back(k, r):
        return spread_copy(r, gb.at[k, member(r)], gp.at[k, g], hs_sem.at[k, r], hr_sem.at[k, r])

    def own_plane(q, _):
        total = plane_sum(yh, 6 * Q + q, q)
        across_copy(q).wait_recv()
        total = total + yrb[q].astype(F32)
        grad[pl.ds(pl.multiple_of(q * R, R), R), :] = total
        k = q // (Q // PARTS)
        first = (q % (Q // PARTS)) * (R // MR)
        gs[k, pl.ds(first, R // MR)] = total.astype(BF16).reshape(R // MR, MR, W)
        return 0

    def moments(value, who, rows, lanes):
        first = f1[who, rows, lanes] + (1.0 - beta_one) * value
        second = f2[who, rows, lanes] + (1.0 - beta_two) * value * value
        step = first / (jnp.sqrt(second) + adam_epsilon)
        return rounded(first), rounded(second), step

    def quantize(values):
        scale = jnp.max(jnp.abs(values), axis=-1, keepdims=True) + block_epsilon
        return (values * (1.0 / scale)).astype(BF16), scale

    def rounded(values):
        codes, scale = quantize(values)
        return codes.astype(F32) * scale

    def own_update(k):
        def body(i, _):
            rows = pl.ds(pl.multiple_of(k * PR + i * MR, MR), MR)
            for b in range(NB):
                lanes = slice(b * BLK, (b + 1) * BLK)
                one, two, step = moments(grad[rows, lanes], 0, rows, lanes)
                mid1[rows, lanes] = one
                mid2[rows, lanes] = two
                upd[rows, lanes] = mm[rows, lanes] - (0.5 * learn_rate) * step
            return 0

        lax.fori_loop(0, NG, body, 0)

    def final_update(k):
        def body(i, _):
            rows = pl.ds(pl.multiple_of(k * PR + i * MR, MR), MR)
            scales = []
            for b in range(NB):
                lanes = slice(b * BLK, (b + 1) * BLK)
                one, two, step = moments(gp[k, i, :, lanes].astype(F32), 1, rows, lanes)
                mo[rows, lanes] = upd[rows, lanes] - (0.5 * learn_rate) * step
                codes, scale = quantize(0.5 * (mid1[rows, lanes] + one))
                c1o[rows, lanes] = codes
                srow[0, rows, b : b + 1] = scale
                codes, scale = quantize(0.5 * (mid2[rows, lanes] + two))
                c2o[rows, lanes] = codes
                srow[0, rows, NB + b : NB + b + 1] = scale
            return 0

        lax.fori_loop(0, NG, body, 0)

    def start_grads(k):
        each_member(lambda r: grad_out(k, r).start())
        gr[k][g] = gs[k, g]

    def pass_grads(k):
        each_member(lambda r: grad_out(k, r).wait_recv())

        def select(h, _):
            gb[k, h] = gr[k][partner_ref[h]]
            return 0

        lax.fori_loop(0, NG, select, 0)
        each_member(lambda r: grad_back(k, r).start())
        gp[k, g] = gb[k, g]

    def outs(k):
        rows = pl.ds(k * PR, PR)
        return [
            pltpu.make_async_copy(mo.at[rows], mo_hbm.at[rows], out_sem.at[k, 0]),
            pltpu.make_async_copy(c1o.at[rows], c1o_hbm.at[rows], out_sem.at[k, 1]),
            pltpu.make_async_copy(c2o.at[rows], c2o_hbm.at[rows], out_sem.at[k, 2]),
        ]

    lax.fori_loop(0, Q // PARTS, own_plane, 0)
    start_grads(0)
    lax.fori_loop(Q // PARTS, Q, own_plane, 0)
    start_grads(1)
    own_update(0)
    pass_grads(0)
    own_update(1)
    pass_grads(1)
    for k in range(PARTS):
        each_member(lambda r: grad_back(k, r).wait_recv())
        final_update(k)
        for c in outs(k):
            c.start()
    so[...] = jnp.transpose(srow[0])
    scale_copies = [
        pltpu.make_async_copy(so.at[pl.ds(0, NB)], so1_hbm, in_sem.at[4]),
        pltpu.make_async_copy(so.at[pl.ds(NB, NB)], so2_hbm, in_sem.at[5]),
    ]
    for c in scale_copies:
        c.start()

    def ring_sent(n, _):
        ring_copy(0, n).wait_send()
        ring_copy(1, n).wait_send()
        return 0

    lax.fori_loop(0, NP, ring_sent, 0)

    def across_sent(q, _):
        across_copy(q).wait_send()
        return 0

    lax.fori_loop(0, Q, across_sent, 0)

    def all_sent(r):
        state_out(r).wait_send()
        scale_out(r).wait_send()
        state_back(r).wait_send()
        for k in range(PARTS):
            grad_out(k, r).wait_send()
            grad_back(k, r).wait_send()

    each_member(all_sent)
    for k in range(PARTS):
        for c in outs(k):
            c.wait()
    for c in scale_copies:
        c.wait()


def per_device(x, c, master, c1, s1, c2, s2, partner):
    anywhere = pl.BlockSpec(memory_space=pl.ANY)
    vm, dma = pltpu.VMEM, pltpu.SemaphoreType.DMA
    mo, c1o, so1, c2o, so2 = pl.pallas_call(
        kernel,
        out_shape=(
            jax.ShapeDtypeStruct((W, W), F32),
            jax.ShapeDtypeStruct((W, W), BF16),
            jax.ShapeDtypeStruct((NB, W), F32),
            jax.ShapeDtypeStruct((W, W), BF16),
            jax.ShapeDtypeStruct((NB, W), F32),
        ),
        in_specs=[pl.BlockSpec(memory_space=pltpu.SMEM)] + [anywhere] * 7,
        out_specs=[anywhere] * 5,
        scratch_shapes=[
            vm((2 * NZ, T, W), BF16), vm((T, W), BF16), vm((NG, SR, W), F32),
            vm((2, NP, R, W), BF16), vm((2, NP, R, W), BF16), vm((Q, R, W), BF16), vm((Q, R, W), BF16),
            vm((NG, 3, SR, W), BF16), vm((NG, 3, SR, W), BF16), vm((NG, 3, SR, W), BF16),
            vm((NG, 3, SR, W), BF16), vm((2 * NB, W), F32), vm((NG, 2 * NB, W), F32),
            vm((2, W, 2 * NB), F32),
            vm((2, W, W), F32), vm((2, W, W), F32), vm((W, W), F32), vm((W, W), F32),
            vm((PARTS, NG, MR, W), BF16), vm((NG, MR, W), BF16), vm((NG, MR, W), BF16),
            vm((PARTS, NG, MR, W), BF16), vm((PARTS, NG, MR, W), BF16),
            vm((W, W), F32), vm((W, W), F32), vm((W, W), F32),
            vm((W, W), F32), vm((W, W), BF16), vm((W, W), BF16), vm((2 * NB, W), F32),
            dma((2 * NZ,)), dma((6,)), dma((PARTS, 3)),
            dma((2, NP)), dma((2, NP)), dma((Q,)), dma((Q,)),
            dma((NG,)), dma((NG,)), dma((NG,)), dma((NG,)), dma((NG,)), dma((NG,)),
            dma((PARTS, NG)), dma((PARTS, NG)), dma((PARTS, NG)), dma((PARTS, NG)),
        ],
        compiler_params=pltpu.CompilerParams(
            collective_id=0, has_side_effects=True, vmem_limit_bytes=67043328
        ),
    )(
        partner, x[0], c[0], master.reshape(NG, SR, W), c1.reshape(NG, SR, W),
        c2.reshape(NG, SR, W), s1[0].T, s2[0].T,
    )
    return (mo[None], c1o[None], so1.T[None], c2o[None], so2.T[None])


def solution(mesh):
    rows = P("group", "fsdp", None)
    return jax.shard_map(
        per_device, mesh=mesh, in_specs=(rows,) * 7 + (P(),), out_specs=(rows,) * 5, check_vma=False
    )
```

time: 357 us -> 120 us (0.34)
  waiting for transfers between devices: 215 us -> 0 us
  Pallas kernels: 0 us -> 111 us
  blocking collectives: 42.7 us -> 0 us
  local copies, waits for them, and re-layouts: 40.4 us -> 8.59 us
  starting transfers between devices: 21.7 us -> 0 us
  matrix products: 14.9 us -> 0 us
  between operations: 14.3 us -> 0.64 us
  other arithmetic: 6.93 us -> 0 us
    all_to_all x3 -> x0, waiting for transfers between devices: 178 us -> none  [the longest x1 157 us: per_device(): lax.all_to_all(inputs, 'fsdp', split_axis=1, concat_axis=0, tiled=True)]
    pallas_call x0 -> x1, Pallas kernels: none -> 111 us  [per_device(): pl.pallas_call(kernel, out_shape=(jax.ShapeDtypeStruct((W, W), F32), jax....]
    all_to_all x1 -> x0, blocking collectives: 42.7 us -> none  [side_by_side_2(): lax.all_to_all(both, axis, split_axis=split_dim, concat_axis=concat_dim,...]
    all_gather x1 -> x0, waiting for transfers between devices: 35.6 us -> none  [per_device(): lax.all_gather(cotangent, 'fsdp', axis=0, tiled=True)]
    all_to_all x3 -> x0, starting transfers between devices: 21.7 us -> none  [the longest x1 11.9 us: per_device(): lax.all_to_all(inputs, 'fsdp', split_axis=1, concat_axis=0, tiled=True)]
    dot_general x4 -> x0, matrix products: 14.9 us -> none  [the longest x1 9.01 us: per_device(): lax.dot_general(columns, lax.all_gather(cotangent, 'fsdp', axis=0, tiled=...]
    all_to_all x1 -> x0, local copies, waits for them, and re-layouts: 8.61 us -> none  [per_device(): lax.all_to_all(inputs, 'fsdp', split_axis=1, concat_axis=0, tiled=True)]
    reshape x5 -> x0, local copies, waits for them, and re-layouts: 7.93 us -> none  [the longest x2 4.58 us: per_device(): gradient_rows = grad.reshape(block_rows, 128)]
  transfers between devices with their start and end apart: 4 -> 0, of which waited for: 4 -> 0; matrix products, arithmetic and copies ran while one was open for 7% -> 0% of each run, Pallas kernels for 0% -> 0%
where the time goes in v1:
time: 120 us
  Pallas kernels  111 us (92%)
  local copies, waits for them, and re-layouts  8.59 us (7%)
    pallas_call x1, Pallas kernels, per_device(): pl.pallas_call(kernel, out_shape=(jax.ShapeDtypeStruct((W, W), F32), jax....  111 us
    unnamed x5, local copies, waits for them, and re-layouts  8.59 us

profile of v1, /device:TPU:1, one launch (start us, length us, event | category | flops | bytes accessed | tf_op | source)
XLA Modules:
  0.0 119.8 jit_solution(17502363669475231904)
XLA Ops:
  0.6 110.6 %shard_map.119 = (f32[512,512]{1,0:T(8,128)}, bf16[512,512]{1,0:T(8,128)(2,1)}, f32[4,512]{1,0:T(4,128)}, bf16[512,512]{1,0:T(8,128)(2,1)}, f32[4,512]{1,0:T(4,128)}) custom-call(s32[16]{0:T(128)} %partner_ref.1, bf16[384,8192]{1,0:T(8,128)(2,1)} %bitcast.20, bf16[384,512]{1,0:T(8,128)(2,1)} %bitcast.27, f32[16,32,512]{2,1,0:T(8,128)} %bitcast.21, ...), custom_call_target="tpu_custom_call" | custom-call | tf_op jit(solution)/shard_map/pallas_call | solution.py:391
  111.2 2.3 %copy.18 = f32[1,512,512]{2,1,0:T(8,128)} copy(f32[1,512,512]{2,1,0:T(8,128)} %bitcast.22) | data formatting | bytes 2097152
  113.5 1.9 %copy.19 = bf16[1,512,512]{2,1,0:T(8,128)(2,1)} copy(bf16[1,512,512]{2,1,0:T(8,128)(2,1)} %bitcast.26) | data formatting | bytes 1048576
  115.4 1.3 %copy.20 = f32[1,512,4]{1,2,0:T(4,128)} copy(f32[1,512,4]{1,2,0:T(4,128)} %bitcast.29) | data formatting | bytes 16384
  116.7 1.9 %copy.21 = bf16[1,512,512]{2,1,0:T(8,128)(2,1)} copy(bf16[1,512,512]{2,1,0:T(8,128)(2,1)} %bitcast.25) | data formatting | bytes 1048576
  118.5 1.3 %copy.22 = f32[1,512,4]{1,2,0:T(4,128)} copy(f32[1,512,4]{1,2,0:T(4,128)} %bitcast.28) | data formatting | bytes 16384

commit v2 on v1

--- a/solution.py
+++ b/solution.py
@@ -19,9 +19,9 @@
 Q = 4
 R = W // Q
 NP = 7 * Q
-PARTS = 2
-PR = W // PARTS
-MR = PR // NG
+MR = 2 * R // NG
+HW = W // 2
+TR = 32
 SR = W // NG
 BLK = 128
 NB = W // BLK
@@ -35,9 +35,9 @@
     mo_hbm, c1o_hbm, so1_hbm, c2o_hbm, so2_hbm,
     xv, cv, mv, sbuf, rbuf, ysb, yrb,
     st, st_r, st_b, st_p, sc, sc_all, srow,
-    f1, f2, mm, grad, gs, gr0, gr1, gb, gp, mid1, mid2, upd,
+    f1, f2, mm, grad, gs, gr0, gr1, gr2, gr3, gb, gp, mid1, mid2, upd,
     mo, c1o, c2o, so,
-    x_sem, in_sem, out_sem, zs_sem, zr_sem, ys_sem, yr_sem,
+    x_sem, xf_sem, in_sem, out_sem, zs_sem, zr_sem, ys_sem, yr_sem,
     ss_sem, sr_sem, cs_sem, cr_sem, ps_sem, pr_sem, gs_sem, gr_sem, hs_sem, hr_sem,
 ):
     g = lax.axis_index("group")
@@ -66,8 +66,15 @@
     ]
     c_in = pltpu.make_async_copy(c_hbm, cv, in_sem.at[0])
     c_in.start()
-    for f in first_chunks:
-        x_copy(f).start()
+
+    def first_copy(way, q):
+        f = first_chunks[way]
+        cols = pl.ds(pl.multiple_of(f * W + q * R, R), R)
+        mine = pl.ds(pl.multiple_of(q * R, R), R)
+        return pltpu.make_async_copy(x_hbm.at[:, cols], xv.at[f, :, mine], xf_sem.at[way, q])
+
+    first_copy(0, 0).start()
+    first_copy(1, 0).start()
     state_in = [
         pltpu.make_async_copy(m_hbm, mv, in_sem.at[1]),
         pltpu.make_async_copy(c1_hbm, st.at[:, 1], in_sem.at[2]),
@@ -78,22 +85,25 @@
     rest = [chunk(yh, (z + 5) % NZ), chunk(y_other, (z + 3) % NZ)]
     for d in (2, 6, 1, 7, 0):
         rest += [chunk(y_other, (z + d) % NZ), chunk(yh, (z + d) % NZ)]
-    for f in rest[:2]:
+
+    barrier = pltpu.get_barrier_semaphore()
+    for d in (up, down, across):
+        pl.semaphore_signal(barrier, inc=1, device_id=d, device_id_type=MESH)
+
+    def greet(r, _):
+        pl.semaphore_signal(barrier, inc=1, device_id=(member(r), f_me), device_id_type=MESH)
+        return 0
+
+    lax.fori_loop(1, NG, greet, 0)
+    for q in range(1, Q):
+        first_copy(0, q).start()
+        first_copy(1, q).start()
+    for f in first_chunks[2:] + rest[:2]:
         x_copy(f).start()
     for c in state_in:
         c.start()
     for f in rest[2:]:
         x_copy(f).start()
-
-    barrier = pltpu.get_barrier_semaphore()
-    for d in (up, down, across):
-        pl.semaphore_signal(barrier, inc=1, device_id=d, device_id_type=MESH)
-
-    def greet(r, _):
-        pl.semaphore_signal(barrier, inc=1, device_id=(member(r), f_me), device_id_type=MESH)
-        return 0
-
-    lax.fori_loop(1, NG, greet, 0)
 
     def partial_grad(f, q):
         cols = pl.ds(pl.multiple_of(q * R, R), R)
@@ -131,6 +141,11 @@
         sbuf[way, n] = total.astype(BF16)
         ring_copy(way, n).start()
 
+    def first_step(n, _):
+        first_copy(0, n).wait()
+        first_copy(1, n).wait()
+        return fresh_step(n, 0)
+
     def fresh_step(n, _):
         ring_piece(0, n, True)
         ring_piece(1, n, True)
@@ -142,10 +157,8 @@
         return 0
 
     c_in.wait()
-    x_copy(first_chunks[0]).wait()
-    x_copy(first_chunks[1]).wait()
     pl.semaphore_wait(barrier, NG + 2)
-    lax.fori_loop(0, Q, fresh_step, 0)
+    lax.fori_loop(0, Q, first_step, 0)
     x_copy(first_chunks[2]).wait()
     x_copy(first_chunks[3]).wait()
     lax.fori_loop(Q, 2 * Q, fresh_step, 0)
@@ -249,7 +262,7 @@
 
     lax.fori_loop(0, Q, other_plane, 0)
 
-    gr = (gr0, gr1)
+    gr = (gr0, gr1, gr2, gr3)
 
     def grad_out(k, r):
         return spread_copy(r, gs.at[k, member(r)], gr[k].at[g], gs_sem.at[k, r], gr_sem.at[k, r])
@@ -257,15 +270,15 @@
     def grad_back(k, r):
         return spread_copy(r, gb.at[k, member(r)], gp.at[k, g], hs_sem.at[k, r], hr_sem.at[k, r])
 
-    def own_plane(q, _):
+    def own_plane(q):
         total = plane_sum(yh, 6 * Q + q, q)
         across_copy(q).wait_recv()
         total = total + yrb[q].astype(F32)
-        grad[pl.ds(pl.multiple_of(q * R, R), R), :] = total
-        k = q // (Q // PARTS)
-        first = (q % (Q // PARTS)) * (R // MR)
-        gs[k, pl.ds(first, R // MR)] = total.astype(BF16).reshape(R // MR, MR, W)
-        return 0
+        grad[q * R : (q + 1) * R, :] = total
+        sent = total.astype(BF16)
+        for j in range(NG):
+            i, h = j // 2, j % 2
+            gs[q, j] = sent[i * MR : (i + 1) * MR, h * HW : (h + 1) * HW]
 
     def moments(value, who, rows, lanes):
         first = f1[who, rows, lanes] + (1.0 - beta_one) * value
@@ -283,7 +296,7 @@
 
     def own_update(k):
         def body(i, _):
-            rows = pl.ds(pl.multiple_of(k * PR + i * MR, MR), MR)
+            rows = pl.ds(pl.multiple_of(k * R + i * TR, TR), TR)
             for b in range(NB):
                 lanes = slice(b * BLK, (b + 1) * BLK)
                 one, two, step = moments(grad[rows, lanes], 0, rows, lanes)
@@ -292,15 +305,22 @@
                 upd[rows, lanes] = mm[rows, lanes] - (0.5 * learn_rate) * step
             return 0
 
-        lax.fori_loop(0, NG, body, 0)
+        lax.fori_loop(0, R // TR, body, 0)
 
     def final_update(k):
         def body(i, _):
-            rows = pl.ds(pl.multiple_of(k * PR + i * MR, MR), MR)
-            scales = []
+            rows = pl.ds(pl.multiple_of(k * R + i * TR, TR), TR)
             for b in range(NB):
                 lanes = slice(b * BLK, (b + 1) * BLK)
-                one, two, step = moments(gp[k, i, :, lanes].astype(F32), 1, rows, lanes)
+                h, first = b // 2, (b % 2) * BLK
+                other = jnp.concatenate(
+                    [
+                        gp[k, 2 * (i * (TR // MR) + u) + h, :, first : first + BLK]
+                        for u in range(TR // MR)
+                    ],
+                    axis=0,
+                )
+                one, two, step = moments(other.astype(F32), 1, rows, lanes)
                 mo[rows, lanes] = upd[rows, lanes] - (0.5 * learn_rate) * step
                 codes, scale = quantize(0.5 * (mid1[rows, lanes] + one))
                 c1o[rows, lanes] = codes
@@ -310,7 +330,7 @@
                 srow[0, rows, NB + b : NB + b + 1] = scale
             return 0
 
-        lax.fori_loop(0, NG, body, 0)
+        lax.fori_loop(0, R // TR, body, 0)
 
     def start_grads(k):
         each_member(lambda r: grad_out(k, r).start())
@@ -328,26 +348,47 @@
         gp[k, g] = gb[k, g]
 
     def outs(k):
-        rows = pl.ds(k * PR, PR)
+        rows = pl.ds(k * R, R)
         return [
             pltpu.make_async_copy(mo.at[rows], mo_hbm.at[rows], out_sem.at[k, 0]),
             pltpu.make_async_copy(c1o.at[rows], c1o_hbm.at[rows], out_sem.at[k, 1]),
             pltpu.make_async_copy(c2o.at[rows], c2o_hbm.at[rows], out_sem.at[k, 2]),
         ]
 
-    lax.fori_loop(0, Q // PARTS, own_plane, 0)
-    start_grads(0)
-    lax.fori_loop(Q // PARTS, Q, own_plane, 0)
-    start_grads(1)
-    own_update(0)
-    pass_grads(0)
-    own_update(1)
-    pass_grads(1)
-    for k in range(PARTS):
+    def finish(k):
         each_member(lambda r: grad_back(k, r).wait_recv())
         final_update(k)
         for c in outs(k):
             c.start()
+
+    def ring_sent(n, _):
+        ring_copy(0, n).wait_send()
+        ring_copy(1, n).wait_send()
+        return 0
+
+    def across_sent(q, _):
+        across_copy(q).wait_send()
+        return 0
+
+    def early_sent(r):
+        state_out(r).wait_send()
+        scale_out(r).wait_send()
+        state_back(r).wait_send()
+
+    for k in range(Q):
+        own_plane(k)
+        start_grads(k)
+        own_update(k)
+        if k >= 1:
+            pass_grads(k - 1)
+        if k >= 2:
+            finish(k - 2)
+    each_member(early_sent)
+    lax.fori_loop(0, Q, across_sent, 0)
+    pass_grads(Q - 1)
+    finish(Q - 2)
+    lax.fori_loop(0, NP, ring_sent, 0)
+    finish(Q - 1)
     so[...] = jnp.transpose(srow[0])
     scale_copies = [
         pltpu.make_async_copy(so.at[pl.ds(0, NB)], so1_hbm, in_sem.at[4]),
@@ -356,39 +397,33 @@
     for c in scale_copies:
         c.start()
 
-    def ring_sent(n, _):
-        ring_copy(0, n).wait_send()
-        ring_copy(1, n).wait_send()
-        return 0
-
-    lax.fori_loop(0, NP, ring_sent, 0)
-
-    def across_sent(q, _):
-        across_copy(q).wait_send()
-        return 0
-
-    lax.fori_loop(0, Q, across_sent, 0)
-
-    def all_sent(r):
-        state_out(r).wait_send()
-        scale_out(r).wait_send()
-        state_back(r).wait_send()
-        for k in range(PARTS):
+    def grads_sent(r):
+        for k in range(Q):
             grad_out(k, r).wait_send()
             grad_back(k, r).wait_send()
 
-    each_member(all_sent)
-    for k in range(PARTS):
+    each_member(grads_sent)
+    for k in range(Q):
         for c in outs(k):
             c.wait()
     for c in scale_copies:
         c.wait()
 
 
+def store_kernel(*refs):
+    ins, outs, sems = refs[:5], refs[5:10], refs[10]
+    copies = [pltpu.make_async_copy(a, b, sems.at[i]) for i, (a, b) in enumerate(zip(ins, outs))]
+    for c in copies:
+        c.start()
+    for c in copies:
+        c.wait()
+
+
 def per_device(x, c, master, c1, s1, c2, s2, partner):
     anywhere = pl.BlockSpec(memory_space=pl.ANY)
+    in_hbm = pl.BlockSpec(memory_space=pltpu.HBM)
     vm, dma = pltpu.VMEM, pltpu.SemaphoreType.DMA
-    mo, c1o, so1, c2o, so2 = pl.pallas_call(
+    results = pl.pallas_call(
         kernel,
         out_shape=(
             jax.ShapeDtypeStruct((W, W), F32),
@@ -397,7 +432,7 @@
             jax.ShapeDtypeStruct((W, W), BF16),
             jax.ShapeDtypeStruct((NB, W), F32),
         ),
-        in_specs=[pl.BlockSpec(memory_space=pltpu.SMEM)] + [anywhere] * 7,
+        in_specs=[pl.BlockSpec(memory_space=pltpu.SMEM)] + [in_hbm] * 7,
         out_specs=[anywhere] * 5,
         scratch_shapes=[
             vm((2 * NZ, T, W), BF16), vm((T, W), BF16), vm((NG, SR, W), F32),
@@ -406,22 +441,35 @@
             vm((NG, 3, SR, W), BF16), vm((2 * NB, W), F32), vm((NG, 2 * NB, W), F32),
             vm((2, W, 2 * NB), F32),
             vm((2, W, W), F32), vm((2, W, W), F32), vm((W, W), F32), vm((W, W), F32),
-            vm((PARTS, NG, MR, W), BF16), vm((NG, MR, W), BF16), vm((NG, MR, W), BF16),
-            vm((PARTS, NG, MR, W), BF16), vm((PARTS, NG, MR, W), BF16),
+            vm((Q, NG, MR, HW), BF16), *(vm((NG, MR, HW), BF16) for _ in range(4)),
+            vm((Q, NG, MR, HW), BF16), vm((Q, NG, MR, HW), BF16),
             vm((W, W), F32), vm((W, W), F32), vm((W, W), F32),
             vm((W, W), F32), vm((W, W), BF16), vm((W, W), BF16), vm((2 * NB, W), F32),
-            dma((2 * NZ,)), dma((6,)), dma((PARTS, 3)),
+            dma((2 * NZ,)), dma((2, Q)), dma((6,)), dma((Q, 3)),
             dma((2, NP)), dma((2, NP)), dma((Q,)), dma((Q,)),
             dma((NG,)), dma((NG,)), dma((NG,)), dma((NG,)), dma((NG,)), dma((NG,)),
-            dma((PARTS, NG)), dma((PARTS, NG)), dma((PARTS, NG)), dma((PARTS, NG)),
+            dma((Q, NG)), dma((Q, NG)), dma((Q, NG)), dma((Q, NG)),
         ],
         compiler_params=pltpu.CompilerParams(
-            collective_id=0, has_side_effects=True, vmem_limit_bytes=67043328
+            collective_id=0, has_side_effects=True, vmem_limit_bytes=46 << 20
         ),
     )(
-        partner, x[0], c[0], master.reshape(NG, SR, W), c1.reshape(NG, SR, W),
-        c2.reshape(NG, SR, W), s1[0].T, s2[0].T,
+        partner, *(
+            pltpu.with_memory_space_constraint(a, pltpu.HBM)
+            for a in (
+                x[0], c[0], master.reshape(NG, SR, W), c1.reshape(NG, SR, W),
+                c2.reshape(NG, SR, W), s1[0].T, s2[0].T,
+            )
+        )
     )
+    mo, c1o, so1, c2o, so2 = pl.pallas_call(
+        store_kernel,
+        out_shape=tuple(jax.ShapeDtypeStruct(a.shape, a.dtype) for a in results),
+        in_specs=[anywhere] * 5,
+        out_specs=[in_hbm] * 5,
+        scratch_shapes=[dma((5,))],
+        compiler_params=pltpu.CompilerParams(vmem_limit_bytes=1 << 20),
+    )(*results)
     return (mo[None], c1o[None], so1.T[None], c2o[None], so2.T[None])
 
 

time: 120 us -> 113 us (0.942)
  local copies, waits for them, and re-layouts: 8.59 us -> 0.65 us
    unnamed x5 -> x2, local copies, waits for them, and re-layouts: 8.59 us -> 0.65 us
    pallas_call x0 -> x1, Pallas kernels: none -> 1.36 us  [per_device(): pl.pallas_call(store_kernel, out_shape=tuple((jax.ShapeDtypeStruct(a.shap...]
where the time goes in v2:
time: 113 us
  Pallas kernels  112 us (99%)
    pallas_call x1, Pallas kernels, per_device(): pl.pallas_call(kernel, out_shape=(jax.ShapeDtypeStruct((W, W), F32), jax....  110 us

profile of v2, /device:TPU:1, one launch (start us, length us, event | category | flops | bytes accessed | tf_op | source)
XLA Modules:
  0.0 112.8 jit_solution(12514180379668965031)
XLA Ops:
  0.6 0.0 copy-start
  0.6 0.6 copy-done
  1.3 110.2 %shard_map.119 = (f32[512,512]{1,0:T(8,128)S(1)}, bf16[512,512]{1,0:T(8,128)(2,1)S(1)}, f32[4,512]{1,0:T(4,128)S(1)}, bf16[512,512]{1,0:T(8,128)(2,1)S(1)}, f32[4,512]{1,0:T(4,128)S(1)}) custom-call(s32[16]{0:T(128)S(1)} %copy-done, bf16[384,8192]{1,0:T(8,128)(2,1)} %bitcast.20, bf16[384,512]{1,0:T(8,128)(2,1)} %bitcast.24, f32[16,32,512]{2,1,0:T(8,128)} %bitcast.21, ...), custom_call_target="tpu_custom_call" | custom-call | tf_op jit(solution)/shard_map/pallas_call | solution.py:426
  111.5 1.4 %shard_map.120 = (f32[512,512]{1,0:T(8,128)}, bf16[512,512]{1,0:T(8,128)(2,1)}, f32[4,512]{1,0:T(4,128)}, bf16[512,512]{1,0:T(8,128)(2,1)}, f32[4,512]{1,0:T(4,128)}) custom-call(f32[512,512]{1,0:T(8,128)S(1)} %get-tuple-element.15.refs_0_, bf16[512,512]{1,0:T(8,128)(2,1)S(1)} %get-tuple-element.16.refs_1_, f32[4,512]{1,0:T(4,128)S(1)} %get-tuple-element.17.refs_2_, ...), custom_call_target="tpu_custom_call" | custom-call | tf_op jit(solution)/shard_map/pallas_call | solution.py:465
Async XLA Ops:
  0.6 0.7 copy-start

commit v3 on v2

--- a/solution.py
+++ b/solution.py
@@ -18,7 +18,10 @@
 W = 512
 Q = 4
 R = W // Q
-NP = 7 * Q
+QB = Q - 1
+RB = 64
+RO = R - RB
+SLOTS = 8 * Q
 MR = 2 * R // NG
 HW = W // 2
 TR = 32
@@ -33,11 +36,11 @@
 def kernel(
     partner_ref, x_hbm, c_hbm, m_hbm, c1_hbm, c2_hbm, s1_hbm, s2_hbm,
     mo_hbm, c1o_hbm, so1_hbm, c2o_hbm, so2_hbm,
-    xv, cv, mv, sbuf, rbuf, ysb, yrb,
+    xv, cv, mv, sbuf, rbuf, ysb, yrb, ybs, ybr,
     st, st_r, st_b, st_p, sc, sc_all, srow,
     f1, f2, mm, grad, gs, gr0, gr1, gr2, gr3, gb, gp, mid1, mid2, upd,
     mo, c1o, c2o, so,
-    x_sem, xf_sem, in_sem, out_sem, zs_sem, zr_sem, ys_sem, yr_sem,
+    x_sem, xf_sem, in_sem, out_sem, zs_sem, zr_sem, ys_sem, yr_sem, bs_sem, br_sem,
     ss_sem, sr_sem, cs_sem, cr_sem, ps_sem, pr_sem, gs_sem, gr_sem, hs_sem, hr_sem,
 ):
     g = lax.axis_index("group")
@@ -111,62 +114,85 @@
             xv[f, :, cols], cv[...], (((0,), (0,)), ((), ())), preferred_element_type=F32
         )
 
-    def ring_copy(way, n):
+    def ring_copy(way, n, rows=R):
+        part = pl.ds(0, rows)
         return pltpu.make_async_remote_copy(
-            src_ref=sbuf.at[way, n], dst_ref=rbuf.at[way, n],
+            src_ref=sbuf.at[way, n, part], dst_ref=rbuf.at[way, n, part],
             send_sem=zs_sem.at[way, n], recv_sem=zr_sem.at[way, n],
             device_id=(up, down)[way], device_id_type=MESH,
         )
 
-    def ring_piece(way, n, fresh):
-        m = n + Q
-        step, p = m // (2 * Q), m % (2 * Q)
-        q, half = p % Q, p // Q
-        d = 4 - step
-        last = step // 3
-        if way == 0:
-            kind = half + (1 - 2 * half) * (1 - last)
-            t = (z + d) % NZ
-            prev = n - 2 * Q + last * (Q - 2 * Q * half)
+    plane_order = (4, 3, 5, 2, 6, 1, 7, 0)
+
+    def plane_copy(i):
+        return pltpu.make_async_remote_copy(
+            src_ref=ybs.at[i], dst_ref=ybr.at[i], send_sem=bs_sem.at[i], recv_sem=br_sem.at[i],
+            device_id=across, device_id_type=MESH,
+        )
+
+    def plane_send(i):
+        t = (z + plane_order[i]) % NZ
+        ybs[i] = partial_grad(chunk(y_other, t), QB)[RO:].astype(BF16)
+        plane_copy(i).start()
+
+    def from_plane(i):
+        plane_copy(i).wait_recv()
+        return ybr[i].astype(F32)
+
+    def slot(d, own, q):
+        return (d - 1) * (2 * Q) + own * Q + q
+
+    def ring_piece(way, d, own, q, last=False):
+        t = (z + d) % NZ if way == 0 else (z + NZ - d) % NZ
+        total = partial_grad(chunk(yh if own else y_other, t), q)
+        n = slot(d, own, q)
+        rows = RO if last and not own else R
+        total = total[:rows]
+        if d < 3 or (d == 3 and own == way):
+            prev = slot(d + 1, own, q)
+            ring_copy(way, prev, rows).wait_recv()
+            total = total + rbuf[way, prev, :rows].astype(F32)
+        if last and own:
+            i = 7 - 2 * d if way == 0 else 8 - 2 * d
+            sbuf[way, n, :RO] = total[:RO].astype(BF16)
+            sbuf[way, n, RO:] = (total[RO:] + from_plane(i)).astype(BF16)
         else:
-            kind = half
-            t = (z + NZ - d) % NZ
-            prev = n - 2 * Q
-        y = yh * kind + y_other * (1 - kind)
-        f = chunk(y, t)
-        total = partial_grad(f, q)
-        if not fresh:
-            ring_copy(way, prev).wait_recv()
-            total = total + rbuf[way, prev].astype(F32)
-        sbuf[way, n] = total.astype(BF16)
-        ring_copy(way, n).start()
-
-    def first_step(n, _):
-        first_copy(0, n).wait()
-        first_copy(1, n).wait()
-        return fresh_step(n, 0)
-
-    def fresh_step(n, _):
-        ring_piece(0, n, True)
-        ring_piece(1, n, True)
-        return 0
-
-    def ring_step(n, _):
-        ring_piece(0, n, False)
-        ring_piece(1, n, False)
-        return 0
+            sbuf[way, n, :rows] = total.astype(BF16)
+        ring_copy(way, n, rows).start()
+
+    def ring_pieces(d, own_up, own_down, begin=0):
+        def body(q, _):
+            ring_piece(0, d, own_up, q)
+            ring_piece(1, d, own_down, q)
+            return 0
+
+        lax.fori_loop(begin, QB, body, 0)
+        ring_piece(0, d, own_up, QB, True)
+        ring_piece(1, d, own_down, QB, True)
 
     c_in.wait()
+    first_copy(0, 0).wait()
+    first_copy(1, 0).wait()
     pl.semaphore_wait(barrier, NG + 2)
-    lax.fori_loop(0, Q, first_step, 0)
-    x_copy(first_chunks[2]).wait()
-    x_copy(first_chunks[3]).wait()
-    lax.fori_loop(Q, 2 * Q, fresh_step, 0)
+    ring_piece(0, 4, 0, 0)
+    ring_piece(1, 4, 1, 0)
+    for q in range(1, Q):
+        first_copy(0, q).wait()
+        first_copy(1, q).wait()
+    plane_send(0)
+    ring_pieces(4, 0, 1, begin=1)
+    for f in first_chunks[2:] + rest[:2]:
+        x_copy(f).wait()
+    plane_send(1)
+    plane_send(2)
+    ring_pieces(3, 1, 0)
+    for f in rest[2:]:
+        x_copy(f).wait()
+    for i in range(3, NZ):
+        plane_send(i)
 
     for c in state_in:
         c.wait()
-    for f in rest:
-        x_copy(f).wait()
 
     def to_bf16(j, _):
         st[j, 0] = mv[j].astype(BF16)
@@ -204,7 +230,8 @@
     st_r[g] = st[g]
     sc_all[g] = sc[...]
 
-    lax.fori_loop(2 * Q, 4 * Q, ring_step, 0)
+    ring_pieces(3, 0, 1)
+    ring_pieces(2, 1, 0)
 
     def state_arrived(r):
         state_out(r).wait_recv()
@@ -220,47 +247,56 @@
     each_member(lambda r: state_back(r).start())
     st_p[g] = st_b[g]
 
-    lax.fori_loop(4 * Q, 5 * Q, ring_step, 0)
-
-    each_member(lambda r: state_back(r).wait_recv())
-    srow[0] = jnp.transpose(sc[...])
-    srow[1] = jnp.transpose(sc_all[partner_ref[g]])
-
-    def prepare(j, _):
-        rows = pl.ds(pl.multiple_of(j * SR, SR), SR)
-        own_s, other_s = srow[0, rows, :], srow[1, rows, :]
-        for b in range(NB):
-            lanes = slice(b * BLK, (b + 1) * BLK)
-            for who, buf, s in ((0, st, own_s), (1, st_p, other_s)):
+    ring_pieces(2, 0, 1)
+
+    def prepare(who, buf):
+        def body(j, _):
+            rows = pl.ds(pl.multiple_of(j * SR, SR), SR)
+            s = srow[who, rows, :]
+            for b in range(NB):
+                lanes = slice(b * BLK, (b + 1) * BLK)
                 f1[who, rows, lanes] = beta_one * (buf[j, 1, :, lanes].astype(F32) * s[:, b : b + 1])
                 f2[who, rows, lanes] = beta_two * (
                     buf[j, 2, :, lanes].astype(F32) * s[:, NB + b : NB + b + 1]
                 )
-        mm[rows, :] = (0.5 * (1.0 - learn_rate * decay_rate)) * (mv[j] + st_p[j, 0].astype(F32))
+            if who == 1:
+                mm[rows, :] = (0.5 * (1.0 - learn_rate * decay_rate)) * (mv[j] + buf[j, 0].astype(F32))
+            return 0
+
+        lax.fori_loop(0, NG, body, 0)
+
+    srow[0] = jnp.transpose(sc[...])
+    srow[1] = jnp.transpose(sc_all[partner_ref[g]])
+    prepare(0, st)
+    ring_pieces(1, 0, 0)
+    ring_pieces(1, 1, 1)
+
+    def across_copy(q, rows=R):
+        part = pl.ds(0, rows)
+        return pltpu.make_async_remote_copy(
+            src_ref=ysb.at[q, part], dst_ref=yrb.at[q, part],
+            send_sem=ys_sem.at[q], recv_sem=yr_sem.at[q], device_id=across, device_id_type=MESH,
+        )
+
+    def plane_sum(own, q, rows):
+        n = slot(1, own, q)
+        total = partial_grad(chunk(yh if own else y_other, z), q)[:rows]
+        ring_copy(0, n, rows).wait_recv()
+        ring_copy(1, n, rows).wait_recv()
+        return total + rbuf[0, n, :rows].astype(F32) + rbuf[1, n, :rows].astype(F32)
+
+    def other_plane(q, rows):
+        ysb[q, :rows] = plane_sum(0, q, rows).astype(BF16)
+        across_copy(q, rows).start()
+
+    def whole_piece(q, _):
+        other_plane(q, R)
         return 0
 
-    lax.fori_loop(0, NG, prepare, 0)
-
-    lax.fori_loop(5 * Q, NP, ring_step, 0)
-
-    def across_copy(q):
-        return pltpu.make_async_remote_copy(
-            src_ref=ysb.at[q], dst_ref=yrb.at[q], send_sem=ys_sem.at[q], recv_sem=yr_sem.at[q],
-            device_id=across, device_id_type=MESH,
-        )
-
-    def plane_sum(y, n, q):
-        total = partial_grad(chunk(y, z), q)
-        ring_copy(0, n).wait_recv()
-        ring_copy(1, n).wait_recv()
-        return total + rbuf[0, n].astype(F32) + rbuf[1, n].astype(F32)
-
-    def other_plane(q, _):
-        ysb[q] = plane_sum(y_other, 5 * Q + q, q).astype(BF16)
-        across_copy(q).start()
-        return 0
-
-    lax.fori_loop(0, Q, other_plane, 0)
+    lax.fori_loop(0, QB, whole_piece, 0)
+    other_plane(QB, RO)
+    each_member(lambda r: state_back(r).wait_recv())
+    prepare(1, st_p)
 
     gr = (gr0, gr1, gr2, gr3)
 
@@ -271,10 +307,13 @@
         return spread_copy(r, gb.at[k, member(r)], gp.at[k, g], hs_sem.at[k, r], hr_sem.at[k, r])
 
     def own_plane(q):
-        total = plane_sum(yh, 6 * Q + q, q)
-        across_copy(q).wait_recv()
-        total = total + yrb[q].astype(F32)
-        grad[q * R : (q + 1) * R, :] = total
+        total = plane_sum(1, q, R)
+        rows = RO if q == QB else R
+        across_copy(q, rows).wait_recv()
+        grad[q * R : q * R + rows, :] = total[:rows] + yrb[q, :rows].astype(F32)
+        if q == QB:
+            grad[W - RB :, :] = total[RO:] + from_plane(7)
+        total = grad[q * R : (q + 1) * R, :]
         sent = total.astype(BF16)
         for j in range(NG):
             i, h = j // 2, j % 2
@@ -361,9 +400,16 @@
         for c in outs(k):
             c.start()
 
-    def ring_sent(n, _):
-        ring_copy(0, n).wait_send()
-        ring_copy(1, n).wait_send()
+    def ring_sent(way, d, own):
+        def body(q, _):
+            ring_copy(way, slot(d, own, q)).wait_send()
+            return 0
+
+        lax.fori_loop(0, QB, body, 0)
+        ring_copy(way, slot(d, own, QB), R if own else RO).wait_send()
+
+    def planes_sent(i, _):
+        plane_copy(i).wait_send()
         return 0
 
     def across_sent(q, _):
@@ -384,10 +430,16 @@
         if k >= 2:
             finish(k - 2)
     each_member(early_sent)
-    lax.fori_loop(0, Q, across_sent, 0)
+    lax.fori_loop(0, QB, across_sent, 0)
+    across_copy(QB, RO).wait_send()
+    lax.fori_loop(0, NZ, planes_sent, 0)
     pass_grads(Q - 1)
     finish(Q - 2)
-    lax.fori_loop(0, NP, ring_sent, 0)
+    for d in (4, 3, 2, 1):
+        for own in (0, 1):
+            for way in (0, 1):
+                if d < 4 or own == way:
+                    ring_sent(way, d, own)
     finish(Q - 1)
     so[...] = jnp.transpose(srow[0])
     scale_copies = [
@@ -436,7 +488,8 @@
         out_specs=[anywhere] * 5,
         scratch_shapes=[
             vm((2 * NZ, T, W), BF16), vm((T, W), BF16), vm((NG, SR, W), F32),
-            vm((2, NP, R, W), BF16), vm((2, NP, R, W), BF16), vm((Q, R, W), BF16), vm((Q, R, W), BF16),
+            vm((2, SLOTS, R, W), BF16), vm((2, SLOTS, R, W), BF16), vm((Q, R, W), BF16), vm((Q, R, W), BF16),
+            vm((NZ, RB, W), BF16), vm((NZ, RB, W), BF16),
             vm((NG, 3, SR, W), BF16), vm((NG, 3, SR, W), BF16), vm((NG, 3, SR, W), BF16),
             vm((NG, 3, SR, W), BF16), vm((2 * NB, W), F32), vm((NG, 2 * NB, W), F32),
             vm((2, W, 2 * NB), F32),
@@ -446,15 +499,15 @@
             vm((W, W), F32), vm((W, W), F32), vm((W, W), F32),
             vm((W, W), F32), vm((W, W), BF16), vm((W, W), BF16), vm((2 * NB, W), F32),
             dma((2 * NZ,)), dma((2, Q)), dma((6,)), dma((Q, 3)),
-            dma((2, NP)), dma((2, NP)), dma((Q,)), dma((Q,)),
+            dma((2, SLOTS)), dma((2, SLOTS)), dma((Q,)), dma((Q,)), dma((NZ,)), dma((NZ,)),
             dma((NG,)), dma((NG,)), dma((NG,)), dma((NG,)), dma((NG,)), dma((NG,)),
             dma((Q, NG)), dma((Q, NG)), dma((Q, NG)), dma((Q, NG)),
         ],
         compiler_params=pltpu.CompilerParams(
-            collective_id=0, has_side_effects=True, vmem_limit_bytes=46 << 20
+            collective_id=0, has_side_effects=True, vmem_limit_bytes=50 << 20
         ),
     )(
-        partner, *(
+        pltpu.with_memory_space_constraint(partner, pltpu.SMEM), *(
             pltpu.with_memory_space_constraint(a, pltpu.HBM)
             for a in (
                 x[0], c[0], master.reshape(NG, SR, W), c1.reshape(NG, SR, W),

time: 113 us -> 108 us (0.956)
  Pallas kernels: 112 us -> 106 us
    pallas_call x1, Pallas kernels: 110 us -> 105 us  [per_device(): pl.pallas_call(kernel, out_shape=(jax.ShapeDtypeStruct((W, W), F32), jax....]
where the time goes in v3:
time: 108 us; the launch traced here: 107 us
  Pallas kernels  106 us (98%)
    pallas_call x1, Pallas kernels, per_device(): pl.pallas_call(kernel, out_shape=(jax.ShapeDtypeStruct((W, W), F32), jax....  105 us

profile of v3, /device:TPU:1, one launch (start us, length us, event | category | flops | bytes accessed | tf_op | source)
XLA Modules:
  0.0 107.4 jit_solution(13873825134602832873)
XLA Ops:
  0.6 0.0 copy-start
  0.6 0.6 copy-done
  1.3 104.8 %shard_map.119 = (f32[512,512]{1,0:T(8,128)S(1)}, bf16[512,512]{1,0:T(8,128)(2,1)S(1)}, f32[4,512]{1,0:T(4,128)S(1)}, bf16[512,512]{1,0:T(8,128)(2,1)S(1)}, f32[4,512]{1,0:T(4,128)S(1)}) custom-call(s32[16]{0:T(128)S(1)} %copy-done, bf16[384,8192]{1,0:T(8,128)(2,1)} %bitcast.20, bf16[384,512]{1,0:T(8,128)(2,1)} %bitcast.24, f32[16,32,512]{2,1,0:T(8,128)} %bitcast.21, ...), custom_call_target="tpu_custom_call" | custom-call | tf_op jit(solution)/shard_map/pallas_call | solution.py:478
  106.1 1.4 %shard_map.120 = (f32[512,512]{1,0:T(8,128)}, bf16[512,512]{1,0:T(8,128)(2,1)}, f32[4,512]{1,0:T(4,128)}, bf16[512,512]{1,0:T(8,128)(2,1)}, f32[4,512]{1,0:T(4,128)}) custom-call(f32[512,512]{1,0:T(8,128)S(1)} %get-tuple-element.15.refs_0_, bf16[512,512]{1,0:T(8,128)(2,1)S(1)} %get-tuple-element.16.refs_1_, f32[4,512]{1,0:T(4,128)S(1)} %get-tuple-element.17.refs_2_, ...), custom_call_target="tpu_custom_call" | custom-call | tf_op jit(solution)/shard_map/pallas_call | solution.py:518
Async XLA Ops:
  0.6 0.7 copy-start

commit v4 on v3

--- a/solution.py
+++ b/solution.py
@@ -19,7 +19,7 @@
 Q = 4
 R = W // Q
 QB = Q - 1
-RB = 64
+RB = 80
 RO = R - RB
 SLOTS = 8 * Q
 MR = 2 * R // NG
@@ -34,13 +34,12 @@
 
 
 def kernel(
-    partner_ref, x_hbm, c_hbm, m_hbm, c1_hbm, c2_hbm, s1_hbm, s2_hbm,
-    mo_hbm, c1o_hbm, so1_hbm, c2o_hbm, so2_hbm,
+    partner_hbm, x_hbm, c_hbm, m_hbm, c1_hbm, c2_hbm, s1_hbm, s2_hbm,
+    mo, c1o, so1, c2o, so2,
     xv, cv, mv, sbuf, rbuf, ysb, yrb, ybs, ybr,
     st, st_r, st_b, st_p, sc, sc_all, srow,
     f1, f2, mm, grad, gs, gr0, gr1, gr2, gr3, gb, gp, mid1, mid2, upd,
-    mo, c1o, c2o, so,
-    x_sem, xf_sem, in_sem, out_sem, zs_sem, zr_sem, ys_sem, yr_sem, bs_sem, br_sem,
+    partner_ref, x_sem, xf_sem, in_sem, zs_sem, zr_sem, ys_sem, yr_sem, bs_sem, br_sem,
     ss_sem, sr_sem, cs_sem, cr_sem, ps_sem, pr_sem, gs_sem, gr_sem, hs_sem, hr_sem,
 ):
     g = lax.axis_index("group")
@@ -84,6 +83,7 @@
         pltpu.make_async_copy(c2_hbm, st.at[:, 2], in_sem.at[3]),
         pltpu.make_async_copy(s1_hbm, sc.at[pl.ds(0, NB)], in_sem.at[4]),
         pltpu.make_async_copy(s2_hbm, sc.at[pl.ds(NB, NB)], in_sem.at[5]),
+        pltpu.make_async_copy(partner_hbm, partner_ref, in_sem.at[6]),
     ]
     rest = [chunk(yh, (z + 5) % NZ), chunk(y_other, (z + 3) % NZ)]
     for d in (2, 6, 1, 7, 0):
@@ -233,6 +233,8 @@
     ring_pieces(3, 0, 1)
     ring_pieces(2, 1, 0)
 
+    ring_pieces(2, 0, 1)
+
     def state_arrived(r):
         state_out(r).wait_recv()
         scale_out(r).wait_recv()
@@ -247,7 +249,6 @@
     each_member(lambda r: state_back(r).start())
     st_p[g] = st_b[g]
 
-    ring_pieces(2, 0, 1)
 
     def prepare(who, buf):
         def body(j, _):
@@ -386,19 +387,9 @@
         each_member(lambda r: grad_back(k, r).start())
         gp[k, g] = gb[k, g]
 
-    def outs(k):
-        rows = pl.ds(k * R, R)
-        return [
-            pltpu.make_async_copy(mo.at[rows], mo_hbm.at[rows], out_sem.at[k, 0]),
-            pltpu.make_async_copy(c1o.at[rows], c1o_hbm.at[rows], out_sem.at[k, 1]),
-            pltpu.make_async_copy(c2o.at[rows], c2o_hbm.at[rows], out_sem.at[k, 2]),
-        ]
-
     def finish(k):
         each_member(lambda r: grad_back(k, r).wait_recv())
         final_update(k)
-        for c in outs(k):
-            c.start()
 
     def ring_sent(way, d, own):
         def body(q, _):
@@ -424,16 +415,17 @@
     for k in range(Q):
         own_plane(k)
         start_grads(k)
-        own_update(k)
         if k >= 1:
             pass_grads(k - 1)
-        if k >= 2:
+        own_update(k)
+        if 2 <= k < Q - 1:
             finish(k - 2)
+    pass_grads(Q - 1)
     each_member(early_sent)
     lax.fori_loop(0, QB, across_sent, 0)
     across_copy(QB, RO).wait_send()
     lax.fori_loop(0, NZ, planes_sent, 0)
-    pass_grads(Q - 1)
+    finish(Q - 3)
     finish(Q - 2)
     for d in (4, 3, 2, 1):
         for own in (0, 1):
@@ -441,13 +433,9 @@
                 if d < 4 or own == way:
                     ring_sent(way, d, own)
     finish(Q - 1)
-    so[...] = jnp.transpose(srow[0])
-    scale_copies = [
-        pltpu.make_async_copy(so.at[pl.ds(0, NB)], so1_hbm, in_sem.at[4]),
-        pltpu.make_async_copy(so.at[pl.ds(NB, NB)], so2_hbm, in_sem.at[5]),
-    ]
-    for c in scale_copies:
-        c.start()
+    scales = jnp.transpose(srow[0])
+    so1[...] = scales[:NB]
+    so2[...] = scales[NB:]
 
     def grads_sent(r):
         for k in range(Q):
@@ -455,11 +443,6 @@
             grad_back(k, r).wait_send()
 
     each_member(grads_sent)
-    for k in range(Q):
-        for c in outs(k):
-            c.wait()
-    for c in scale_copies:
-        c.wait()
 
 
 def store_kernel(*refs):
@@ -484,8 +467,8 @@
             jax.ShapeDtypeStruct((W, W), BF16),
             jax.ShapeDtypeStruct((NB, W), F32),
         ),
-        in_specs=[pl.BlockSpec(memory_space=pltpu.SMEM)] + [in_hbm] * 7,
-        out_specs=[anywhere] * 5,
+        in_specs=[in_hbm] * 8,
+        out_specs=[pl.BlockSpec(memory_space=pltpu.VMEM)] * 5,
         scratch_shapes=[
             vm((2 * NZ, T, W), BF16), vm((T, W), BF16), vm((NG, SR, W), F32),
             vm((2, SLOTS, R, W), BF16), vm((2, SLOTS, R, W), BF16), vm((Q, R, W), BF16), vm((Q, R, W), BF16),
@@ -497,8 +480,7 @@
             vm((Q, NG, MR, HW), BF16), *(vm((NG, MR, HW), BF16) for _ in range(4)),
             vm((Q, NG, MR, HW), BF16), vm((Q, NG, MR, HW), BF16),
             vm((W, W), F32), vm((W, W), F32), vm((W, W), F32),
-            vm((W, W), F32), vm((W, W), BF16), vm((W, W), BF16), vm((2 * NB, W), F32),
-            dma((2 * NZ,)), dma((2, Q)), dma((6,)), dma((Q, 3)),
+            pltpu.SMEM((NG,), jnp.int32), dma((2 * NZ,)), dma((2, Q)), dma((7,)),
             dma((2, SLOTS)), dma((2, SLOTS)), dma((Q,)), dma((Q,)), dma((NZ,)), dma((NZ,)),
             dma((NG,)), dma((NG,)), dma((NG,)), dma((NG,)), dma((NG,)), dma((NG,)),
             dma((Q, NG)), dma((Q, NG)), dma((Q, NG)), dma((Q, NG)),
@@ -507,10 +489,10 @@
             collective_id=0, has_side_effects=True, vmem_limit_bytes=50 << 20
         ),
     )(
-        pltpu.with_memory_space_constraint(partner, pltpu.SMEM), *(
+        *(
             pltpu.with_memory_space_constraint(a, pltpu.HBM)
             for a in (
-                x[0], c[0], master.reshape(NG, SR, W), c1.reshape(NG, SR, W),
+                partner, x[0], c[0], master.reshape(NG, SR, W), c1.reshape(NG, SR, W),
                 c2.reshape(NG, SR, W), s1[0].T, s2[0].T,
             )
         )

time: 108 us -> 104 us (0.963)
  Pallas kernels: 106 us -> 103 us
    pallas_call x1, Pallas kernels: 105 us -> 102 us  [per_device(): pl.pallas_call(kernel, out_shape=(jax.ShapeDtypeStruct((W, W), F32), jax....]
where the time goes in v4:
time: 104 us
  Pallas kernels  103 us (99%)
    pallas_call x1, Pallas kernels, per_device(): pl.pallas_call(kernel, out_shape=(jax.ShapeDtypeStruct((W, W), F32), jax....  102 us

profile of v4, /device:TPU:1, one launch (start us, length us, event | category | flops | bytes accessed | tf_op | source)
XLA Modules:
  0.0 104.0 jit_solution(7302816795293766778)
XLA Ops:
  0.6 102.0 %shard_map.119 = (f32[512,512]{1,0:T(8,128)S(1)}, bf16[512,512]{1,0:T(8,128)(2,1)S(1)}, f32[4,512]{1,0:T(4,128)S(1)}, bf16[512,512]{1,0:T(8,128)(2,1)S(1)}, f32[4,512]{1,0:T(4,128)S(1)}) custom-call(s32[16]{0:T(128)} %partner_hbm.1, bf16[384,8192]{1,0:T(8,128)(2,1)} %bitcast.20, bf16[384,512]{1,0:T(8,128)(2,1)} %bitcast.24, f32[16,32,512]{2,1,0:T(8,128)} %bitcast.21, ...), custom_call_target="tpu_custom_call" | custom-call | tf_op jit(solution)/shard_map/pallas_call | solution.py:461
  102.6 1.4 %shard_map.120 = (f32[512,512]{1,0:T(8,128)}, bf16[512,512]{1,0:T(8,128)(2,1)}, f32[4,512]{1,0:T(4,128)}, bf16[512,512]{1,0:T(8,128)(2,1)}, f32[4,512]{1,0:T(4,128)}) custom-call(f32[512,512]{1,0:T(8,128)S(1)} %get-tuple-element.15.refs_0_, bf16[512,512]{1,0:T(8,128)(2,1)S(1)} %get-tuple-element.16.refs_1_, f32[4,512]{1,0:T(4,128)S(1)} %get-tuple-element.17.refs_2_, ...), custom_call_target="tpu_custom_call" | custom-call | tf_op jit(solution)/shard_map/pallas_call | solution.py:500
